TPU v7x, 32 devices: a whole 2x2x4 slice. The times are simulated.
32 devices in a mesh: hour: 2 (over y), pair: 4 (over z), freq: 2 (over x), sub: 2 (over core).
Axes of the slice: x: 2, y: 2, z: 4, core: 2. Of those that a mesh axis runs over, the one named last changes fastest.
Arguments:
- raw: float32 [512, 4096], P('freq', ('hour', 'pair', 'sub')), parts along dimension 1, may hold values from -60 to 60
- offsets: int32 [16], P(('hour', 'pair', 'sub')), parts along dimension 0, may hold values from 0 to 255
- pair_mask: int32 [4, 2], P('pair'), may hold values 0 or 1
Outputs:
- correlations: bfloat16 [8, 3, 128, 128, 256], P(('hour', 'pair'), None, 'sub', 'freq'), parts along dimension 0
There are 2 independent parts, one for each index of `hour`. A program takes and returns all parts, laid end to end along the dimension named above; an argument that names none is the same for every part. Nothing has to cross between parts.
All inputs are finite; a program needn't handle non-finite values. No bound on the sum of `pair_mask` on one device may be relied on, other than what follows from the above.
Results may differ from a plain program's by a relative error of at most 0.0056.
Values may be sent and summed in bfloat16 or wider, within the bound.
No kernel may reach another device: no remote copies, remote signals or barrier semaphores. Data moves between devices by JAX's collectives and lax.ppermute only.
A program may use at most 64 MiB of HBM per device.

v0:
```python
import math
import jax
import jax.numpy as jnp
from jax import lax
from jax.sharding import PartitionSpec as P

F = 256
REACH = 2
LAGS = 256
STEP = 256


def shifted(value, axis, steps):
    count = lax.axis_size(axis)
    initial, last = (max(0, -steps), min(count, count - steps))
    return lax.ppermute(value, axis, [(source, source + steps) for source in range(initial, last)])


def dft_basis(freqs, imaginary, span):
    samples = jnp.arange(span, dtype=jnp.int32)
    phase = samples[:, None] * freqs[None, :] % span
    angle = 2.0 * math.pi / span * phase.astype(jnp.float32)
    values = jnp.where(imaginary[None, :], -jnp.sin(angle), jnp.cos(angle)) / math.sqrt(span)
    return values.astype(jnp.bfloat16)


def lag_basis(freqs, imaginary, span, lag_count, bins):
    delays = jnp.arange(lag_count, dtype=jnp.int32) - lag_count // 2
    phase = freqs[:, None] * delays[None, :] % span
    angle = 2.0 * math.pi / span * phase.astype(jnp.float32)
    values = jnp.where(imaginary[:, None], -jnp.sin(angle), jnp.cos(angle)) / math.sqrt(bins)
    return values.astype(jnp.bfloat16)


def tapered(windows):
    span = windows.shape[-1]
    centred = windows - jnp.mean(windows, axis=-1, keepdims=True)
    power = jnp.mean(centred * centred, axis=-1, keepdims=True)
    ticks = jnp.arange(span, dtype=jnp.float32)
    hann_taper = 0.5 - 0.5 * jnp.cos(2.0 * math.pi / span * ticks)
    return (centred * lax.rsqrt(power + 1e-05) * hann_taper).astype(jnp.bfloat16)


def cross_spectra(left, right, factor):
    row_count = left.shape[0]
    col_count = right.shape[0]
    bins = left.shape[3]
    turned = jnp.stack([left[:, :, 1], -left[:, :, 0]], axis=2)
    real_part = jnp.einsum("rwtf,cwtf->rcf", left, right, preferred_element_type=jnp.float32)
    imaginary_part = jnp.einsum("rwtf,cwtf->rcf", turned, right, preferred_element_type=jnp.float32)
    joined = jnp.stack([real_part, imaginary_part], axis=2)
    return joined.reshape(row_count, col_count, 2 * bins) * factor


def body(raw, offsets, pair_mask):
    span = 2 * F
    freq_count = lax.axis_size("freq")
    segment = raw.shape[1]
    extra = (span + segment - 1) // segment
    pieces = [raw]
    for ahead in range(1, extra + 1):
        pieces.append(shifted(raw, ("pair", "sub"), -ahead))
    record = jnp.concatenate(pieces, axis=1)
    starts = jnp.arange(offsets.shape[0], dtype=jnp.int32) * STEP + offsets
    windows = jax.vmap(lambda begin: lax.dynamic_slice_in_dim(record, begin, span, 1), out_axes=1)(
        starts
    )
    column = jnp.arange(span, dtype=jnp.int32)
    freqs = column % F
    imaginary = column >= F
    basis = dft_basis(freqs, imaginary, span)
    spectra = jnp.dot(tapered(windows), basis, preferred_element_type=jnp.float32).astype(
        jnp.bfloat16
    )
    spectra = spectra.reshape(spectra.shape[0], spectra.shape[1], 2, F)
    halves = lax.all_to_all(
        lax.all_to_all(spectra, "freq", split_axis=3, concat_axis=0, tiled=True),
        ("pair", "sub"),
        split_axis=0,
        concat_axis=1,
        tiled=True,
    )
    block = lax.all_gather(halves, "sub", axis=0, tiled=True)
    factor = 1.0 / halves.shape[1]
    full_block = lax.all_gather(block, "freq", axis=3, tiled=True)
    row_count = halves.shape[0]
    rows = lax.dynamic_slice_in_dim(full_block, lax.axis_index("sub") * row_count, row_count, 0)
    col_count = full_block.shape[0] // freq_count
    own_columns = lax.dynamic_slice_in_dim(
        full_block, lax.axis_index("freq") * col_count, col_count, 0
    )
    lag_table = lag_basis(freqs, imaginary, span, LAGS, F)

    def transform(partner):
        term = cross_spectra(rows, partner, factor).astype(jnp.bfloat16)
        return jnp.einsum(
            "pcf,fl->pcl", term, lag_table, preferred_element_type=jnp.float32
        ).astype(jnp.bfloat16)

    def silent(unused):
        return jnp.zeros((row_count, col_count, LAGS), jnp.bfloat16)

    outputs = [transform(own_columns)]
    for offset in range(1, REACH + 1):
        partner = shifted(own_columns, "pair", -offset)
        outputs.append(lax.cond(pair_mask[0, offset - 1] == 1, transform, silent, partner))
    result = jnp.stack(outputs)
    return result[None]


def solution(mesh):
    return jax.shard_map(
        body,
        mesh=mesh,
        in_specs=(P("freq", ("hour", "pair", "sub")), P(("hour", "pair", "sub")), P("pair", None)),
        out_specs=P(("hour", "pair"), None, "sub", "freq", None),
        check_vma=False,
    )
```

profile of v0, /device:TPU:16, one launch (start us, length us, event | category | flops | bytes accessed | tf_op | source)
XLA Modules:
  0.0 169.7 jit_solution(11203225285981303011)
XLA Ops:
  6.5 2.5 %collective-permute-start.1 = (f32[256,256]{1,0:T(8,128)}, f32[256,256]{1,0:T(8,128)S(1)}, u32[]{:S(2)}, u32[]{:S(2)}) collective-permute-start(f32[256,256]{1,0:T(8,128)} %param.7), channel_id=1, source_target_pairs={{4,0},{5,1},{8,4},{9,5},{12,8},{13,9},{6,2},{7,3},{10,6},{11,7},{1... | collective-permute-start | bytes 786440 | tf_op jit(solution)/shard_map/ppermute | solution.py:16
  9.0 1.9 %collective-permute-start = (f32[256,256]{1,0:T(8,128)}, f32[256,256]{1,0:T(8,128)S(1)}, u32[]{:S(2)}, u32[]{:S(2)}) collective-permute-start(f32[256,256]{1,0:T(8,128)} %param.7), channel_id=1, source_target_pairs={{1,0},{4,1},{5,4},{8,5},{9,8},{12,9},{13,12},{3,2},{6,3},{7,6},{10... | collective-permute-start | bytes 786440 | tf_op jit(solution)/shard_map/ppermute | solution.py:16
  11.7 5.1 %collective-permute-done.1 = f32[256,256]{1,0:T(8,128)S(1)} collective-permute-done((f32[256,256]{1,0:T(8,128)}, f32[256,256]{1,0:T(8,128)S(1)}, u32[]{:S(2)}, u32[]{:S(2)}) %collective-permute-start.1) | collective-permute-done | bytes 262176 | tf_op jit(solution)/shard_map/ppermute | solution.py:16
  16.8 0.9 collective-permute-done
  17.7 1.4 fusion.57
  19.1 0.2 fusion.30
  19.4 4.5 %convolution_convert_fusion = bf16[256,512]{1,0:T(8,128)(2,1)S(1)} fusion(s32[512]{0:T(512)S(1)} %add_select_fusion.2, pred[512]{0:T(512)(128)(4,1)S(1)} %iota_compare_fusion, f32[256,512]{1,0:T(8,128)S(1)} %get-tuple-element.49, f32[512]{0:T(512)S(1)} %multiply_subtract_fusion, f32[256]{0:T(256)S(1)} %add_rsqrt_fusion, f32[256]{0:T(256)S(1)} %broadcast_multiply_fusion), kind=kOutput, calls=%fused_computation.31 | convolution fusion | flops 139591680 | bytes 793088 | tf_op jit(solution)/shard_map/dot_general | solution.py:72
  23.9 0.1 reshape.146
  23.9 0.5 copy.29
  24.5 8.6 %all_to_all.36 = bf16[256,1,2,256]{0,2,1,3:T(2,128)(2,1)S(1)} all-to-all(bf16[256,1,2,256]{0,2,1,3:T(2,128)(2,1)S(1)} %copy.29), channel_id=1, replica_groups=mesh['hour'=2,'pair'=4,'freq'=2,'sub'=2] {'freq'}, dimensions={3} | all-to-all | bytes 524288 | tf_op jit(solution)/shard_map/all_to_all | solution.py:77
  33.1 0.2 copy.31
  33.2 0.3 copy.32
  33.5 10.5 %all_to_all.37 = bf16[512,1,2,128]{3,2,1,0:T(2,128)(2,1)S(1)} all-to-all(bf16[512,1,2,128]{3,2,1,0:T(2,128)(2,1)S(1)} %copy.32), channel_id=1, replica_groups=mesh['hour'=2,'pair'=4,'freq'=2,'sub'=2] {'pair','sub'}, dimensions={0} | all-to-all | bytes 524288 | tf_op jit(solution)/shard_map/all_to_all | solution.py:76
  44.1 2.3 %all-gather = bf16[128,8,1,2,128]{4,0,1,3,2:T(8,128)(2,1)} all-gather(bf16[64,8,1,2,128]{4,0,1,3,2:T(8,128)(2,1)S(1)} %bitcast.102), channel_id=2, replica_groups=mesh['hour'=2,'pair'=4,'freq'=2,'sub'=2] {'sub'}, dimensions={0}, use_global_device_ids=true | all-gather | bytes 786432 | tf_op jit(solution)/shard_map/all_gather | solution.py:83
  46.4 0.0 all-gather.4.cloned.1.call-update
  46.5 0.7 fusion.62
  48.5 2.6 %multiply_convert_fusion.2 = bf16[512,256]{1,0:T(8,128)(2,1)S(1)} fusion(s32[256]{0:T(256)S(1)} %iota_add_fusion, s32[512]{0:T(512)S(1)} %add_select_fusion.2, pred[512]{0:T(512)(128)(4,1)S(1)} %iota_compare_fusion), kind=kLoop, calls=%fused_computation.61 | loop fusion | flops 2359296 | bytes 265728 | tf_op jit(solution)/shard_map/convert_element_type | solution.py:32
  51.1 17.5 %all-gather.4.cloned.1.call-done = bf16[128,8,1,2,256]{4,0,1,3,2:T(8,128)(2,1)} async-done(((bf16[128,8,1,2,128]{4,0,1,3,2:T(8,128)(2,1)}), bf16[128,8,1,2,256]{4,0,1,3,2:T(8,128)(2,1)}) %all-gather.4.cloned.1.call-update) | async-done | bytes 1048592 | tf_op jit(solution)/shard_map/all_gather | solution.py:85
  68.6 1.3 constant_dynamic-slice_fusion
  69.9 1.1 copy.37
  71.0 2.4 %collective-permute-start.3 = (bf16[64,8,2,256]{3,1,2,0:T(8,128)(2,1)}, bf16[64,8,2,256]{3,1,2,0:T(8,128)(2,1)S(1)}, u32[]{:S(2)}, u32[]{:S(2)}) collective-permute-start(bf16[64,8,2,256]{3,1,2,0:T(8,128)(2,1)} %copy.37), channel_id=1, source_target_pairs={{8,0},{12,4},{9,1},{13,5},{10,2},{14,6},{11,3},{15,7},{24,16},{28,... | collective-permute-start | bytes 1572872 | tf_op jit(solution)/shard_map/ppermute | solution.py:16
  73.5 2.1 %collective-permute-start.2 = (bf16[64,8,2,256]{3,1,2,0:T(8,128)(2,1)}, bf16[64,8,2,256]{3,1,2,0:T(8,128)(2,1)}, u32[]{:S(2)}, u32[]{:S(2)}) collective-permute-start(bf16[64,8,2,256]{3,1,2,0:T(8,128)(2,1)} %copy.37), channel_id=1, source_target_pairs={{4,0},{8,4},{12,8},{5,1},{9,5},{13,9},{6,2},{10,6},{14,10},{7,3},{... | collective-permute-start | bytes 1572872 | tf_op jit(solution)/shard_map/ppermute | solution.py:16
  75.6 1.0 copy.34
  76.5 1.0 copy.35
  77.5 0.1 fusion.61
  77.6 1.4 convolution_bitcast_fusion.5
  79.0 1.4 convolution_bitcast_fusion.4
  80.4 4.6 %fusion.12 = bf16[64,64,2,256]{0,1,3,2:T(8,128)(2,1)} fusion(f32[64,64,1,256]{0,1,3,2:T(8,128)S(1)} %convolution_bitcast_fusion.4, f32[64,64,1,256]{0,1,3,2:T(8,128)S(1)} %convolution_bitcast_fusion.5), kind=kLoop, calls=%fused_computation.23 | loop fusion | flops 6291456 | bytes 12582912 | tf_op jit(solution)/shard_map/convert_element_type | solution.py:95
  85.0 12.0 %copy.36 = bf16[64,64,512]{2,1,0:T(8,128)(2,1)} copy(bf16[64,64,512]{0,1,2:T(8,128)(2,1)} %bitcast.98) | data formatting | bytes 8388608 | tf_op jit(solution)/shard_map/convert_element_type | solution.py:95
  97.0 7.0 %convert_bitcast_fusion.2 = bf16[1,64,64,256]{3,2,1,0:T(8,128)(2,1)} fusion(bf16[64,64,512]{2,1,0:T(8,128)(2,1)} %copy.36, s32[256]{0:T(256)S(1)} %iota_add_fusion, s32[512]{0:T(512)S(1)} %add_select_fusion.2, pred[512]{0:T(512)(128)(4,1)S(1)} %iota_compare_fusion), kind=kOutput, calls=%fused_computation.27 | convolution fusion | flops 1077149696 | bytes 6295040 | tf_op jit(solution)/shard_map/pcf,fl->pcl/dot_general | solution.py:96
  104.0 24.2 %conditional.3 = (bf16[1,64,64,256]{3,2,1,0:T(8,128)(2,1)S(1)}) conditional(s32[]{:T(128)} %bitcast.42, () %tuple.23, (bf16[64,8,2,256]{3,1,2,0:T(8,128)(2,1)S(1)}, bf16[64,8,2,256]{0,1,2,3:T(8,128)(2,1)S(1)}, bf16[512,256]{1,0:T(8,128)(2,1)S(1)}) %tuple.44), branch_computations={%region_4.5_spmd, %region_5.6_spmd} | conditional | flops 1148583936 | bytes 40108040 | solution.py:106
  104.0 1.3 copy.40
  105.3 0.1 fusion.60
  105.4 1.4 convolution_bitcast_fusion.2
  106.8 1.4 convolution_bitcast_fusion.3
  108.2 4.6 %fusion.6 = bf16[64,64,2,256]{0,1,3,2:T(8,128)(2,1)} fusion(f32[64,64,1,256]{0,1,3,2:T(8,128)S(1)} %convolution_bitcast_fusion.2, f32[64,64,1,256]{0,1,3,2:T(8,128)S(1)} %convolution_bitcast_fusion.3), kind=kLoop, calls=%fused_computation.12 | loop fusion | flops 6291456 | bytes 12582912 | tf_op jit(solution)/shard_map/cond/branch_1_fun/convert_element_type | solution.py:95
  112.8 12.0 %copy.28 = bf16[64,64,512]{2,1,0:T(8,128)(2,1)} copy(bf16[64,64,512]{0,1,2:T(8,128)(2,1)} %bitcast.99) | data formatting | bytes 8388608 | tf_op jit(solution)/shard_map/cond/branch_1_fun/convert_element_type | solution.py:95
  124.8 3.4 %convert_bitcast_fusion.1 = bf16[1,64,64,256]{3,2,1,0:T(8,128)(2,1)S(1)} fusion(bf16[64,64,512]{2,1,0:T(8,128)(2,1)} %copy.28, bf16[512,256]{1,0:T(8,128)(2,1)S(1)} %get-tuple-element.30), kind=kOutput, calls=%fused_computation.15 | convolution fusion | flops 1074790400 | bytes 6553600 | tf_op jit(solution)/shard_map/cond/branch_1_fun/pcf,fl->pcl/dot_general | solution.py:96
  128.2 1.3 copy-done
  129.6 26.9 %conditional.2 = (bf16[1,64,64,256]{3,2,1,0:T(8,128)(2,1)}) conditional(s32[]{:T(128)} %bitcast.40, () %tuple.21, (bf16[64,8,2,256]{3,1,2,0:T(8,128)(2,1)}, bf16[64,8,2,256]{0,1,2,3:T(8,128)(2,1)S(1)}, bf16[512,256]{1,0:T(8,128)(2,1)S(1)}) %tuple.45), branch_computations={%region_2.3_spmd, %region_3.4_spmd} | conditional | flops 1148583936 | bytes 40108040 | solution.py:106
  129.6 2.6 %copy.38 = bf16[64,8,2,256]{0,1,2,3:T(8,128)(2,1)S(1)} copy(bf16[64,8,2,256]{3,1,2,0:T(8,128)(2,1)} %get-tuple-element.42) | data formatting | bytes 1048576 | tf_op jit(solution)/shard_map
  132.2 0.1 fusion.59
  132.3 1.4 convolution_bitcast_fusion
  133.7 1.4 convolution_bitcast_fusion.1
  135.1 4.6 %fusion = bf16[64,64,2,256]{0,1,3,2:T(8,128)(2,1)} fusion(f32[64,64,1,256]{0,1,3,2:T(8,128)S(1)} %convolution_bitcast_fusion, f32[64,64,1,256]{0,1,3,2:T(8,128)S(1)} %convolution_bitcast_fusion.1), kind=kLoop, calls=%fused_computation.1 | loop fusion | flops 6291456 | bytes 12582912 | tf_op jit(solution)/shard_map/cond/branch_1_fun/convert_element_type | solution.py:95
  139.7 12.0 %copy.26 = bf16[64,64,512]{2,1,0:T(8,128)(2,1)} copy(bf16[64,64,512]{0,1,2:T(8,128)(2,1)} %bitcast.100) | data formatting | bytes 8388608 | tf_op jit(solution)/shard_map/cond/branch_1_fun/convert_element_type | solution.py:95
  151.7 4.8 %convert_bitcast_fusion = bf16[1,64,64,256]{3,2,1,0:T(8,128)(2,1)} fusion(bf16[64,64,512]{2,1,0:T(8,128)(2,1)} %copy.26, bf16[512,256]{1,0:T(8,128)(2,1)S(1)} %get-tuple-element.27), kind=kOutput, calls=%fused_computation.4 | convolution fusion | flops 1074790400 | bytes 6553600 | tf_op jit(solution)/shard_map/cond/branch_1_fun/pcf,fl->pcl/dot_general | solution.py:96
  156.5 6.4 %maximum_bitcast_fusion = bf16[1,3,64,64,256]{4,3,2,1,0:T(8,128)(2,1)} fusion(bf16[1,64,64,256]{3,2,1,0:T(8,128)(2,1)} %copy-done, bf16[1,64,64,256]{3,2,1,0:T(8,128)(2,1)} %get-tuple-element.60, bf16[1,64,64,256]{3,2,1,0:T(8,128)(2,1)} %convert_bitcast_fusion.2), kind=kLoop, calls=%fused_computation.24 | loop fusion | flops 6291456 | bytes 12582912 | tf_op jit(solution)/shard_map/broadcast_in_dim | solution.py:108
  (14 shorter events, 0.2 us)
Async XLA Ops:
  6.5 39.9 %copy-start.1 = (s32[1,2]{1,0:T(1,128)S(1)}, s32[1,2]{1,0:T(1,128)}, u32[]{:S(2)}) copy-start(s32[1,2]{1,0:T(1,128)} %param.9) | copy-start | bytes 28
  6.5 62.1 %all-gather.4.cloned.1.call-start = ((), (), s32[]{:S(2)}) async-start(), calls=%async_computation.2 | async-start | bytes 1572864 | tf_op jit(solution)/shard_map/all_gather | solution.py:85
  6.5 10.3 %collective-permute-start.1 = (f32[256,256]{1,0:T(8,128)}, f32[256,256]{1,0:T(8,128)S(1)}, u32[]{:S(2)}, u32[]{:S(2)}) collective-permute-start(f32[256,256]{1,0:T(8,128)} %param.7), channel_id=1, source_target_pairs={{4,0},{5,1},{8,4},{9,5},{12,8},{13,9},{6,2},{7,3},{10,6},{11,7},{1... | collective-permute-start | bytes 786440 | tf_op jit(solution)/shard_map/ppermute | solution.py:16
  9.0 8.7 %collective-permute-start = (f32[256,256]{1,0:T(8,128)}, f32[256,256]{1,0:T(8,128)S(1)}, u32[]{:S(2)}, u32[]{:S(2)}) collective-permute-start(f32[256,256]{1,0:T(8,128)} %param.7), channel_id=1, source_target_pairs={{1,0},{4,1},{5,4},{8,5},{9,8},{12,9},{13,12},{3,2},{6,3},{7,6},{10... | collective-permute-start | bytes 786440 | tf_op jit(solution)/shard_map/ppermute | solution.py:16
  71.0 33.0 %collective-permute-start.3 = (bf16[64,8,2,256]{3,1,2,0:T(8,128)(2,1)}, bf16[64,8,2,256]{3,1,2,0:T(8,128)(2,1)S(1)}, u32[]{:S(2)}, u32[]{:S(2)}) collective-permute-start(bf16[64,8,2,256]{3,1,2,0:T(8,128)(2,1)} %copy.37), channel_id=1, source_target_pairs={{8,0},{12,4},{9,1},{13,5},{10,2},{14,6},{11,3},{15,7},{24,16},{28,... | collective-permute-start | bytes 1572872 | tf_op jit(solution)/shard_map/ppermute | solution.py:16
  73.5 54.8 %collective-permute-start.2 = (bf16[64,8,2,256]{3,1,2,0:T(8,128)(2,1)}, bf16[64,8,2,256]{3,1,2,0:T(8,128)(2,1)}, u32[]{:S(2)}, u32[]{:S(2)}) collective-permute-start(bf16[64,8,2,256]{3,1,2,0:T(8,128)(2,1)} %copy.37), channel_id=1, source_target_pairs={{4,0},{8,4},{12,8},{5,1},{9,5},{13,9},{6,2},{10,6},{14,10},{7,3},{... | collective-permute-start | bytes 1572872 | tf_op jit(solution)/shard_map/ppermute | solution.py:16
  128.2 1.3 copy-start
Sparse Core Ops, SparseCore 0:
  46.6 22.0 all-gather.3
where the time goes:
time: 171 us; the launch traced here: 170 us
  local copies, waits for them, and re-layouts  47.2 us (28%)
  matrix products  27.9 us (16%)
  other arithmetic  25 us (15%)
  waiting for transfers between devices  23.5 us (14%)
  blocking collectives  21.4 us (13%)
  between operations  15.6 us (9%)
  starting transfers between devices  8.95 us (5%)
    convert_element_type x3, local copies, waits for them, and re-layouts, transform(): term = cross_spectra(rows, partner, factor).astype(jnp.bfloat16)  35.9 us
    all_gather x1, waiting for transfers between devices, body(): full_block = lax.all_gather(block, 'freq', axis=3, tiled=True)  17.5 us
    dot_general x3, matrix products, transform(): jnp.einsum('pcf,fl->pcl', term, lag_table, preferred_element_type=jnp.flo...  15.2 us
    convert_element_type x3, other arithmetic, transform(): term = cross_spectra(rows, partner, factor).astype(jnp.bfloat16)  13.9 us
    all_to_all x1, blocking collectives, body(): lax.all_to_all(lax.all_to_all(spectra, 'freq', split_axis=3, concat_axis=...  10.5 us
    ppermute x4, starting transfers between devices, shifted(): lax.ppermute(value, axis, [(source, source + steps) for source in range(i...  8.95 us
    all_to_all x1, blocking collectives, body(): lax.all_to_all(spectra, 'freq', split_axis=3, concat_axis=0, tiled=True)  8.58 us
    broadcast_in_dim x1, other arithmetic, body(): return result[None]  6.38 us
  transfers between devices with their start and end apart: 5, of which 3 were waited for; matrix products, arithmetic and copies ran while one was open for 33% of the time, Pallas kernels for 0%

commit v1 on v0

--- a/solution.py
+++ b/solution.py
@@ -8,6 +8,18 @@
 REACH = 2
 LAGS = 256
 STEP = 256
+
+
+def collect(x, axis, dim):
+    ways, here = (lax.axis_size(axis), lax.axis_index(axis))
+    grown, reach = (x, 1)
+    while reach < ways:
+        theirs = lax.ppermute(grown, axis, [(d, d ^ reach) for d in range(ways)])
+        mine_first = jnp.concatenate([grown, theirs], axis=dim)
+        theirs_first = jnp.concatenate([theirs, grown], axis=dim)
+        grown = jnp.where(here & reach == 0, mine_first, theirs_first)
+        reach = 2 * reach
+    return grown
 
 
 def shifted(value, axis, steps):
@@ -82,7 +94,7 @@
     )
     block = lax.all_gather(halves, "sub", axis=0, tiled=True)
     factor = 1.0 / halves.shape[1]
-    full_block = lax.all_gather(block, "freq", axis=3, tiled=True)
+    full_block = collect(block, "freq", 3)
     row_count = halves.shape[0]
     rows = lax.dynamic_slice_in_dim(full_block, lax.axis_index("sub") * row_count, row_count, 0)
     col_count = full_block.shape[0] // freq_count

time: 171 us -> 157 us (0.918)
  between operations: 15.6 us -> 2.11 us
  waiting for transfers between devices: 23.5 us -> 18 us
  starting transfers between devices: 8.95 us -> 11.8 us
    all_gather x1 -> x0, waiting for transfers between devices: 17.5 us -> none  [body(): full_block = lax.all_gather(block, 'freq', axis=3, tiled=True)]
    ppermute x0 -> x1, waiting for transfers between devices: none -> 9.36 us  [collect(): theirs = lax.ppermute(grown, axis, [(d, d ^ reach) for d in range(ways)])]
    ppermute x4, starting transfers between devices: 8.95 us -> 11.7 us  [shifted(): lax.ppermute(value, axis, [(source, source + steps) for source in range(i...]
    ppermute x4, waiting for transfers between devices: 6.02 us -> 8.64 us  [shifted(): lax.ppermute(value, axis, [(source, source + steps) for source in range(i...]
  transfers between devices with their start and end apart: 5 -> 5, of which waited for: 3 -> 3; matrix products, arithmetic and copies ran while one was open for 33% -> 36% of each run, Pallas kernels for 0% -> 0%
where the time goes in v1:
time: 157 us; the launch traced here: 156 us
  local copies, waits for them, and re-layouts  47.8 us (30%)
  matrix products  29.1 us (19%)
  other arithmetic  26.3 us (17%)
  blocking collectives  20.3 us (13%)
  waiting for transfers between devices  18 us (11%)
  starting transfers between devices  11.8 us (8%)
  between operations  2.11 us (1%)
    convert_element_type x3, local copies, waits for them, and re-layouts, transform(): term = cross_spectra(rows, partner, factor).astype(jnp.bfloat16)  35.9 us
    dot_general x3, matrix products, transform(): jnp.einsum('pcf,fl->pcl', term, lag_table, preferred_element_type=jnp.flo...  15.2 us
    convert_element_type x3, other arithmetic, transform(): term = cross_spectra(rows, partner, factor).astype(jnp.bfloat16)  13.8 us
    ppermute x4, starting transfers between devices, shifted(): lax.ppermute(value, axis, [(source, source + steps) for source in range(i...  11.7 us
    all_to_all x1, blocking collectives, body(): lax.all_to_all(lax.all_to_all(spectra, 'freq', split_axis=3, concat_axis=...  10.4 us
    ppermute x1, waiting for transfers between devices, collect(): theirs = lax.ppermute(grown, axis, [(d, d ^ reach) for d in range(ways)])  9.36 us
    ppermute x4, waiting for transfers between devices, shifted(): lax.ppermute(value, axis, [(source, source + steps) for source in range(i...  8.64 us
    all_to_all x1, blocking collectives, body(): lax.all_to_all(spectra, 'freq', split_axis=3, concat_axis=0, tiled=True)  7.73 us
  transfers between devices with their start and end apart: 5, of which 3 were waited for; matrix products, arithmetic and copies ran while one was open for 36% of the time, Pallas kernels for 0%

profile of v1, /device:TPU:16, one launch (start us, length us, event | category | flops | bytes accessed | tf_op | source)
XLA Modules:
  0.0 155.5 jit_solution(10606547645614035090)
XLA Ops:
  0.0 2.0 %collective-permute-start = (f32[256,256]{1,0:T(8,128)}, f32[256,256]{1,0:T(8,128)S(1)}, u32[]{:S(2)}, u32[]{:S(2)}) collective-permute-start(f32[256,256]{1,0:T(8,128)} %param.7), channel_id=1, source_target_pairs={{1,0},{4,1},{5,4},{8,5},{9,8},{12,9},{13,12},{3,2},{6,3},{7,6},{10... | collective-permute-start | bytes 786440 | tf_op jit(solution)/shard_map/ppermute | solution.py:28
  2.1 2.4 %collective-permute-start.1 = (f32[256,256]{1,0:T(8,128)}, f32[256,256]{1,0:T(8,128)S(1)}, u32[]{:S(2)}, u32[]{:S(2)}) collective-permute-start(f32[256,256]{1,0:T(8,128)} %param.7), channel_id=1, source_target_pairs={{4,0},{5,1},{8,4},{9,5},{12,8},{13,9},{6,2},{7,3},{10,6},{11,7},{1... | collective-permute-start | bytes 786440 | tf_op jit(solution)/shard_map/ppermute | solution.py:28
  5.1 2.0 %collective-permute-done = f32[256,256]{1,0:T(8,128)S(1)} collective-permute-done((f32[256,256]{1,0:T(8,128)}, f32[256,256]{1,0:T(8,128)S(1)}, u32[]{:S(2)}, u32[]{:S(2)}) %collective-permute-start) | collective-permute-done | bytes 262176 | tf_op jit(solution)/shard_map/ppermute | solution.py:28
  7.1 6.6 %collective-permute-done.1 = f32[256,256]{1,0:T(8,128)S(1)} collective-permute-done((f32[256,256]{1,0:T(8,128)}, f32[256,256]{1,0:T(8,128)S(1)}, u32[]{:S(2)}, u32[]{:S(2)}) %collective-permute-start.1) | collective-permute-done | bytes 262176 | tf_op jit(solution)/shard_map/ppermute | solution.py:28
  13.8 1.4 fusion.54
  15.2 0.2 fusion.28
  15.5 4.5 %convolution_convert_fusion = bf16[256,512]{1,0:T(8,128)(2,1)S(1)} fusion(s32[512]{0:T(512)S(1)} %add_select_fusion.2, pred[512]{0:T(512)(128)(4,1)S(1)} %iota_compare_fusion, f32[256,512]{1,0:T(8,128)S(1)} %get-tuple-element.55, f32[512]{0:T(512)S(1)} %multiply_subtract_fusion, f32[256]{0:T(256)S(1)} %add_rsqrt_fusion, f32[256]{0:T(256)S(1)} %broadcast_multiply_fusion), kind=kOutput, calls=%fused_computation.31 | convolution fusion | flops 139591680 | bytes 793088 | tf_op jit(solution)/shard_map/dot_general | solution.py:84
  19.9 0.1 reshape.146
  20.0 0.5 copy.35
  20.5 7.7 %all_to_all.36 = bf16[256,1,2,256]{0,2,1,3:T(2,128)(2,1)S(1)} all-to-all(bf16[256,1,2,256]{0,2,1,3:T(2,128)(2,1)S(1)} %copy.35), channel_id=1, replica_groups=mesh['hour'=2,'pair'=4,'freq'=2,'sub'=2] {'freq'}, dimensions={3} | all-to-all | bytes 524288 | tf_op jit(solution)/shard_map/all_to_all | solution.py:89
  28.3 0.3 copy.36
  28.6 10.4 %all_to_all.37 = bf16[512,1,2,128]{3,2,1,0:T(2,128)(2,1)S(1)} all-to-all(bf16[512,1,2,128]{3,2,1,0:T(2,128)(2,1)S(1)} %bitcast.95), channel_id=1, replica_groups=mesh['hour'=2,'pair'=4,'freq'=2,'sub'=2] {'pair','sub'}, dimensions={0} | all-to-all | bytes 524288 | tf_op jit(solution)/shard_map/all_to_all | solution.py:88
  39.1 0.2 copy.38
  39.2 2.2 %all-gather = bf16[128,8,1,2,128]{4,1,3,2,0:T(8,128)(2,1)S(1)} all-gather(bf16[64,8,1,2,128]{4,1,3,2,0:T(8,128)(2,1)S(1)} %copy.38), channel_id=2, replica_groups=mesh['hour'=2,'pair'=4,'freq'=2,'sub'=2] {'sub'}, dimensions={0}, use_global_device_ids=true | all-gather | bytes 786432 | tf_op jit(solution)/shard_map/all_gather | solution.py:95
  41.4 0.7 copy.39
  42.2 0.1 collective-permute-start.2
  42.3 0.6 fusion.58
  44.2 2.6 %multiply_convert_fusion.2 = bf16[512,256]{1,0:T(8,128)(2,1)S(1)} fusion(s32[256]{0:T(256)S(1)} %iota_add_fusion, s32[512]{0:T(512)S(1)} %add_select_fusion.2, pred[512]{0:T(512)(128)(4,1)S(1)} %iota_compare_fusion), kind=kLoop, calls=%fused_computation.60 | loop fusion | flops 2359296 | bytes 265728 | tf_op jit(solution)/shard_map/convert_element_type | solution.py:44
  46.8 9.4 %collective-permute-done.2 = bf16[128,8,2,128]{0,1,2,3:T(8,128)(2,1)S(1)} collective-permute-done((bf16[128,8,2,128]{0,1,2,3:T(8,128)(2,1)S(1)}, bf16[128,8,2,128]{0,1,2,3:T(8,128)(2,1)S(1)}, u32[]{:S(2)}, u32[]{:S(2)}) %collective-permute-start.2) | collective-permute-done | bytes 524320 | tf_op jit(solution)/shard_map/ppermute | solution.py:17
  56.2 0.2 maximum_select_fusion
  56.4 0.6 constant_dynamic-slice_fusion.1
  57.0 2.2 %copy.41 = bf16[64,8,2,256]{3,1,2,0:T(8,128)(2,1)} copy(bf16[64,8,2,256]{0,1,2,3:T(8,128)(2,1)S(1)} %get-tuple-element.63) | data formatting | bytes 1048576 | tf_op jit(solution)/shard_map/dynamic_slice | solution.py:101
  59.2 3.8 %collective-permute-start.3 = (bf16[64,8,2,256]{3,1,2,0:T(8,128)(2,1)}, bf16[64,8,2,256]{3,1,2,0:T(8,128)(2,1)}, u32[]{:S(2)}, u32[]{:S(2)}) collective-permute-start(bf16[64,8,2,256]{3,1,2,0:T(8,128)(2,1)} %copy.41), channel_id=1, source_target_pairs={{4,0},{8,4},{12,8},{5,1},{9,5},{13,9},{6,2},{10,6},{14,10},{7,3},{... | collective-permute-start | bytes 1572872 | tf_op jit(solution)/shard_map/ppermute | solution.py:28
  63.0 3.5 %collective-permute-start.4 = (bf16[64,8,2,256]{3,1,2,0:T(8,128)(2,1)}, bf16[64,8,2,256]{3,1,2,0:T(8,128)(2,1)}, u32[]{:S(2)}, u32[]{:S(2)}) collective-permute-start(bf16[64,8,2,256]{3,1,2,0:T(8,128)(2,1)} %copy.41), channel_id=1, source_target_pairs={{8,0},{12,4},{9,1},{13,5},{10,2},{14,6},{11,3},{15,7},{24,16},{28,... | collective-permute-start | bytes 1572872 | tf_op jit(solution)/shard_map/ppermute | solution.py:28
  66.5 1.4 convolution_bitcast_fusion.5
  67.9 0.4 constant_dynamic-slice_fusion
  68.2 1.4 convolution_bitcast_fusion.4
  69.6 4.6 %fusion.12 = bf16[64,64,2,256]{0,1,3,2:T(8,128)(2,1)} fusion(f32[64,64,1,256]{0,1,3,2:T(8,128)S(1)} %convolution_bitcast_fusion.4, f32[64,64,1,256]{0,1,3,2:T(8,128)S(1)} %convolution_bitcast_fusion.5), kind=kLoop, calls=%fused_computation.23 | loop fusion | flops 6291456 | bytes 12582912 | tf_op jit(solution)/shard_map/convert_element_type | solution.py:107
  74.2 12.0 %copy.40 = bf16[64,64,512]{2,1,0:T(8,128)(2,1)} copy(bf16[64,64,512]{0,1,2:T(8,128)(2,1)} %bitcast.89) | data formatting | bytes 8388608 | tf_op jit(solution)/shard_map/convert_element_type | solution.py:107
  86.2 7.0 %convert_bitcast_fusion.2 = bf16[1,64,64,256]{3,2,1,0:T(8,128)(2,1)} fusion(bf16[64,64,512]{2,1,0:T(8,128)(2,1)} %copy.40, s32[256]{0:T(256)S(1)} %iota_add_fusion, s32[512]{0:T(512)S(1)} %add_select_fusion.2, pred[512]{0:T(512)(128)(4,1)S(1)} %iota_compare_fusion), kind=kOutput, calls=%fused_computation.27 | convolution fusion | flops 1077149696 | bytes 6295040 | tf_op jit(solution)/shard_map/pcf,fl->pcl/dot_general | solution.py:108
  93.2 25.6 %conditional.2 = (bf16[1,64,64,256]{3,2,1,0:T(8,128)(2,1)S(1)}) conditional(s32[]{:T(128)} %bitcast.39, () %tuple.21, (bf16[64,8,2,256]{3,1,2,0:T(8,128)(2,1)}, bf16[64,8,2,256]{0,1,2,3:T(8,128)(2,1)S(1)}, bf16[512,256]{1,0:T(8,128)(2,1)S(1)}) %tuple.22), branch_computations={%region_2.3_spmd, %region_3.4_spmd} | conditional | flops 1148583936 | bytes 40108040 | solution.py:118
  93.2 0.1 fusion.56
  93.3 2.6 %copy.42 = bf16[64,8,2,256]{0,1,2,3:T(8,128)(2,1)S(1)} copy(bf16[64,8,2,256]{3,1,2,0:T(8,128)(2,1)} %get-tuple-element.48) | data formatting | bytes 1048576 | tf_op jit(solution)/shard_map
  96.0 1.4 convolution_bitcast_fusion
  97.3 1.4 convolution_bitcast_fusion.1
  98.7 4.6 %fusion = bf16[64,64,2,256]{0,1,3,2:T(8,128)(2,1)} fusion(f32[64,64,1,256]{0,1,3,2:T(8,128)S(1)} %convolution_bitcast_fusion, f32[64,64,1,256]{0,1,3,2:T(8,128)S(1)} %convolution_bitcast_fusion.1), kind=kLoop, calls=%fused_computation.1 | loop fusion | flops 6291456 | bytes 12582912 | tf_op jit(solution)/shard_map/cond/branch_1_fun/convert_element_type | solution.py:107
  103.3 12.0 %copy.32 = bf16[64,64,512]{2,1,0:T(8,128)(2,1)} copy(bf16[64,64,512]{0,1,2:T(8,128)(2,1)} %bitcast.90) | data formatting | bytes 8388608 | tf_op jit(solution)/shard_map/cond/branch_1_fun/convert_element_type | solution.py:107
  115.3 3.4 %convert_bitcast_fusion = bf16[1,64,64,256]{3,2,1,0:T(8,128)(2,1)S(1)} fusion(bf16[64,64,512]{2,1,0:T(8,128)(2,1)} %copy.32, bf16[512,256]{1,0:T(8,128)(2,1)S(1)} %get-tuple-element.27), kind=kOutput, calls=%fused_computation.4 | convolution fusion | flops 1074790400 | bytes 6553600 | tf_op jit(solution)/shard_map/cond/branch_1_fun/pcf,fl->pcl/dot_general | solution.py:108
  118.8 1.3 copy-done
  120.1 29.1 %conditional.3 = (bf16[1,64,64,256]{3,2,1,0:T(8,128)(2,1)}) conditional(s32[]{:T(128)} %bitcast.40, () %tuple.23, (bf16[64,8,2,256]{3,1,2,0:T(8,128)(2,1)}, bf16[64,8,2,256]{0,1,2,3:T(8,128)(2,1)S(1)}, bf16[512,256]{1,0:T(8,128)(2,1)S(1)}) %tuple.24), branch_computations={%region_4.5_spmd, %region_5.6_spmd} | conditional | flops 1148583936 | bytes 40108040 | solution.py:118
  120.1 1.1 fusion.57
  121.2 2.6 %copy.44 = bf16[64,8,2,256]{0,1,2,3:T(8,128)(2,1)S(1)} copy(bf16[64,8,2,256]{3,1,2,0:T(8,128)(2,1)} %get-tuple-element.51) | data formatting | bytes 1048576 | tf_op jit(solution)/shard_map
  123.8 2.6 %convolution_bitcast_fusion.2 = f32[64,64,1,256]{0,1,3,2:T(8,128)S(1)} fusion(bf16[64,8,2,256]{0,1,2,3:T(8,128)(2,1)S(1)} %copy.44, bf16[64,8,1,256]{0,1,2,3:T(8,128)(2,1)} %get-tuple-element.59, bf16[64,8,1,256]{0,1,2,3:T(8,128)(2,1)} %get-tuple-element.58), kind=kOutput, calls=%fused_computation.13 | convolution fusion | flops 33816576 | bytes 5242880 | tf_op jit(solution)/shard_map/cond/branch_1_fun/rwtf,cwtf->rcf/dot_general | solution.py:62
  126.4 1.4 convolution_bitcast_fusion.3
  127.8 4.6 %fusion.6 = bf16[64,64,2,256]{0,1,3,2:T(8,128)(2,1)} fusion(f32[64,64,1,256]{0,1,3,2:T(8,128)S(1)} %convolution_bitcast_fusion.2, f32[64,64,1,256]{0,1,3,2:T(8,128)S(1)} %convolution_bitcast_fusion.3), kind=kLoop, calls=%fused_computation.12 | loop fusion | flops 6291456 | bytes 12582912 | tf_op jit(solution)/shard_map/cond/branch_1_fun/convert_element_type | solution.py:107
  132.4 12.0 %copy.34 = bf16[64,64,512]{2,1,0:T(8,128)(2,1)} copy(bf16[64,64,512]{0,1,2:T(8,128)(2,1)} %bitcast.91) | data formatting | bytes 8388608 | tf_op jit(solution)/shard_map/cond/branch_1_fun/convert_element_type | solution.py:107
  144.4 4.8 %convert_bitcast_fusion.1 = bf16[1,64,64,256]{3,2,1,0:T(8,128)(2,1)} fusion(bf16[64,64,512]{2,1,0:T(8,128)(2,1)} %copy.34, bf16[512,256]{1,0:T(8,128)(2,1)S(1)} %get-tuple-element.30), kind=kOutput, calls=%fused_computation.15 | convolution fusion | flops 1074790400 | bytes 6553600 | tf_op jit(solution)/shard_map/cond/branch_1_fun/pcf,fl->pcl/dot_general | solution.py:108
  149.1 6.4 %maximum_bitcast_fusion = bf16[1,3,64,64,256]{4,3,2,1,0:T(8,128)(2,1)} fusion(bf16[1,64,64,256]{3,2,1,0:T(8,128)(2,1)} %get-tuple-element.67, bf16[1,64,64,256]{3,2,1,0:T(8,128)(2,1)} %copy-done, bf16[1,64,64,256]{3,2,1,0:T(8,128)(2,1)} %convert_bitcast_fusion.2), kind=kLoop, calls=%fused_computation.24 | loop fusion | flops 6291456 | bytes 12582912 | tf_op jit(solution)/shard_map/broadcast_in_dim | solution.py:120
  (12 shorter events, 0.1 us)
Async XLA Ops:
  0.0 42.3 %copy-start.1 = (s32[1,2]{1,0:T(1,128)S(1)}, s32[1,2]{1,0:T(1,128)}, u32[]{:S(2)}) copy-start(s32[1,2]{1,0:T(1,128)} %param.9) | copy-start | bytes 28
  0.0 7.1 %collective-permute-start = (f32[256,256]{1,0:T(8,128)}, f32[256,256]{1,0:T(8,128)S(1)}, u32[]{:S(2)}, u32[]{:S(2)}) collective-permute-start(f32[256,256]{1,0:T(8,128)} %param.7), channel_id=1, source_target_pairs={{1,0},{4,1},{5,4},{8,5},{9,8},{12,9},{13,12},{3,2},{6,3},{7,6},{10... | collective-permute-start | bytes 786440 | tf_op jit(solution)/shard_map/ppermute | solution.py:28
  2.1 11.7 %collective-permute-start.1 = (f32[256,256]{1,0:T(8,128)}, f32[256,256]{1,0:T(8,128)S(1)}, u32[]{:S(2)}, u32[]{:S(2)}) collective-permute-start(f32[256,256]{1,0:T(8,128)} %param.7), channel_id=1, source_target_pairs={{4,0},{5,1},{8,4},{9,5},{12,8},{13,9},{6,2},{7,3},{10,6},{11,7},{1... | collective-permute-start | bytes 786440 | tf_op jit(solution)/shard_map/ppermute | solution.py:28
  42.2 14.0 %collective-permute-start.2 = (bf16[128,8,2,128]{0,1,2,3:T(8,128)(2,1)S(1)}, bf16[128,8,2,128]{0,1,2,3:T(8,128)(2,1)S(1)}, u32[]{:S(2)}, u32[]{:S(2)}) collective-permute-start(bf16[128,8,2,128]{0,1,2,3:T(8,128)(2,1)S(1)} %bitcast.92), channel_id=1, source_target_pairs={{0,2},{2,0},{1,3},{3,1},{4,6},{6,4},{5,7},{7,5},{8,10},{10,8},{9,1... | collective-permute-start | bytes 1572872 | tf_op jit(solution)/shard_map/ppermute | solution.py:17
  59.2 34.0 %collective-permute-start.3 = (bf16[64,8,2,256]{3,1,2,0:T(8,128)(2,1)}, bf16[64,8,2,256]{3,1,2,0:T(8,128)(2,1)}, u32[]{:S(2)}, u32[]{:S(2)}) collective-permute-start(bf16[64,8,2,256]{3,1,2,0:T(8,128)(2,1)} %copy.41), channel_id=1, source_target_pairs={{4,0},{8,4},{12,8},{5,1},{9,5},{13,9},{6,2},{10,6},{14,10},{7,3},{... | collective-permute-start | bytes 1572872 | tf_op jit(solution)/shard_map/ppermute | solution.py:28
  63.0 55.8 %collective-permute-start.4 = (bf16[64,8,2,256]{3,1,2,0:T(8,128)(2,1)}, bf16[64,8,2,256]{3,1,2,0:T(8,128)(2,1)}, u32[]{:S(2)}, u32[]{:S(2)}) collective-permute-start(bf16[64,8,2,256]{3,1,2,0:T(8,128)(2,1)} %copy.41), channel_id=1, source_target_pairs={{8,0},{12,4},{9,1},{13,5},{10,2},{14,6},{11,3},{15,7},{24,16},{28,... | collective-permute-start | bytes 1572872 | tf_op jit(solution)/shard_map/ppermute | solution.py:28
  118.8 1.3 copy-start
